TPU v7x, 256 devices: a whole 4x4x8 slice. The times are simulated.
256 devices in a mesh: pb: 64 (over x, y, z_lo), col: 4 (over z_hi, core).
Axes of the slice: x: 4, y: 4, z: 8 (z_hi: 2, z_lo: 4; z = z_hi * 4 + z_lo), core: 2. Of those that a mesh axis runs over, the one named last changes fastest.
Arguments:
- vertex: bfloat16 [3, 256, 448, 896], P(None, 'pb', 'col'), may hold values from -6 to 6
- loop_blocks: bfloat16 [3, 256, 448, 896], P(None, ('pb', 'col')), may hold values from -0.013671875 to 0.013671875
- mixing: float32 [6, 256], replicated, may hold values from -1 to 1
- bond_offsets: int32 [7, 3], replicated, may hold values from -1 to 1
Outputs:
- new_vertex: bfloat16 [3, 256, 448, 896], P(None, 'pb', 'col')
All inputs are finite; a program needn't handle non-finite values.
Results may differ from a plain program's by a relative error of at most 0.007.
Values may be sent and summed in bfloat16 or wider, within the bound.
No kernel may reach another device: no remote copies, remote signals or barrier semaphores. Data moves between devices by JAX's collectives and lax.ppermute only.
A program may use at most 64 MiB of HBM per device.

v0:
```python
import math
import jax
import jax.numpy as jnp
from jax import lax
from jax.sharding import PartitionSpec as P

NB = 7
MX = 8
step_length = 0.25


def mesh_coords(momenta, mesh_y, mesh_z):
    flat_index = jnp.arange(momenta, dtype=jnp.int32)
    coord_x = flat_index // (mesh_y * mesh_z)
    coord_y = flat_index // mesh_z % mesh_y
    coord_z = flat_index % mesh_z
    return (coord_x, coord_y, coord_z)


def phase_tables(momenta, mesh_x, mesh_y, mesh_z):
    coord_x, coord_y, coord_z = mesh_coords(momenta, mesh_y, mesh_z)
    phase_index = (
        coord_x[:, None] * coord_x[None, :] * (mesh_y * mesh_z)
        + coord_y[:, None] * coord_y[None, :] * (mesh_x * mesh_z)
        + coord_z[:, None] * coord_z[None, :] * (mesh_x * mesh_y)
    ) % momenta
    angles = phase_index.astype(jnp.float32) * (2.0 * math.pi / momenta)
    cosine = jnp.cos(angles)
    sine_part = jnp.sin(angles)
    forward = jnp.stack([jnp.stack([cosine, sine_part], 1), jnp.stack([-sine_part, cosine], 1)]) * (
        1.0 / momenta
    )
    backward = jnp.stack([jnp.stack([cosine, -sine_part], 1), jnp.stack([sine_part, cosine], 1)])
    return (forward.astype(jnp.bfloat16), backward.astype(jnp.bfloat16))


def shifted_weights(mixing, bond_offsets, momenta, mesh_x, mesh_y, mesh_z):
    coord_x, coord_y, coord_z = mesh_coords(momenta, mesh_y, mesh_z)
    offsets = bond_offsets[:, None, :] - bond_offsets[None, :, :]
    shift_x = jnp.mod(coord_x[None, None, :] + offsets[:, :, 0:1], mesh_x)
    shift_y = jnp.mod(coord_y[None, None, :] + offsets[:, :, 1:2], mesh_y)
    shift_z = jnp.mod(coord_z[None, None, :] + offsets[:, :, 2:3], mesh_z)
    flat_slot = (shift_x * mesh_y + shift_y) * mesh_z + shift_z
    return jnp.take(mixing, flat_slot, axis=1)


def complex_batch(left_op, right_op):
    half_n = left_op.shape[1]
    real_part = jnp.einsum(
        "bij,bjk->bik", left_op[:, :, :half_n], right_op, preferred_element_type=jnp.float32
    )
    imag_part = jnp.einsum(
        "bij,bjk->bik", left_op[:, :, half_n:], right_op, preferred_element_type=jnp.float32
    )
    return jnp.concatenate(
        [
            real_part[:, :, :half_n] - imag_part[:, :, half_n:],
            real_part[:, :, half_n:] + imag_part[:, :, :half_n],
        ],
        axis=2,
    )


def per_device(vertex, loop_blocks, mixing, bond_offsets):
    groups = lax.axis_size("pb")
    mesh_z = vertex.shape[1]
    row_count = vertex.shape[2]
    full_order = vertex.shape[3] // 2
    narrow = full_order // groups
    momenta = mesh_z * groups
    mesh_y = groups // MX
    forward, backward = phase_tables(momenta, MX, mesh_y, mesh_z)
    weights = shifted_weights(mixing, bond_offsets, momenta, MX, mesh_y, mesh_z)
    split_cols = vertex.reshape(3, mesh_z, row_count, 2, full_order)
    gathered = lax.all_to_all(split_cols, "pb", split_axis=4, concat_axis=1, tiled=True)
    lattice = lax.dot_general(
        gathered, forward, (((3, 1), (0, 1)), ((), ())), preferred_element_type=jnp.float32
    )
    lattice = lax.optimization_barrier(lattice.astype(jnp.bfloat16)).astype(jnp.float32)
    blocks = lattice.reshape(3, row_count // NB, NB, narrow // NB, NB, 2, momenta)
    mixed_list = []
    for target in range(3):
        first_w = weights[2 * target][None, :, None, :, None, :]
        second_w = weights[2 * target + 1][None, :, None, :, None, :]
        summed = first_w * blocks[(target + 1) % 3] + second_w * blocks[(target + 2) % 3]
        mixed_list.append(summed.astype(jnp.bfloat16).reshape(row_count, narrow, 2, momenta))
    mixed_all = jnp.stack(mixed_list)
    projected = jnp.einsum(
        "tanpr,prsq->tqasn", mixed_all, backward, preferred_element_type=jnp.float32
    ).astype(jnp.bfloat16)
    returned_proj = lax.all_to_all(projected, "pb", split_axis=1, concat_axis=4, tiled=True)
    returned_proj = returned_proj.reshape(3, mesh_z, row_count, 2 * full_order)
    united_rows = (vertex.astype(jnp.float32) + returned_proj.astype(jnp.float32)).astype(
        jnp.bfloat16
    )
    united = lax.all_to_all(united_rows, "col", split_axis=1, concat_axis=2, tiled=True)
    local_q = united.shape[1]
    flat_united = united.reshape(3 * local_q, full_order, 2 * full_order)
    flat_loops = loop_blocks.reshape(3 * local_q, full_order, 2 * full_order)
    middle = complex_batch(flat_united, flat_loops).astype(jnp.bfloat16)
    change = complex_batch(middle, flat_united)
    increment = (
        (step_length * change).astype(jnp.bfloat16).reshape(3, local_q, full_order, 2 * full_order)
    )
    returned = lax.all_to_all(increment, "col", split_axis=2, concat_axis=1, tiled=True)
    return (vertex.astype(jnp.float32) + returned.astype(jnp.float32)).astype(jnp.bfloat16)


def solution(mesh):
    return jax.shard_map(
        per_device,
        mesh=mesh,
        in_specs=(P(None, "pb", "col", None), P(None, ("pb", "col"), None, None), P(), P()),
        out_specs=P(None, "pb", "col", None),
        check_vma=False,
    )
```

profile of v0, /device:TPU:32, one launch (start us, length us, event | category | flops | bytes accessed | tf_op | source)
XLA Modules:
  0.0 358.5 jit_solution(17212420372139971582)
XLA Ops:
  0.0 8.3 %reshape.772 = bf16[3,4,112,2,448]{4,3,2,1,0:T(2,128)(2,1)} reshape(bf16[3,4,112,896]{3,2,1,0:T(8,128)(2,1)} %param.4) | data formatting | bytes 4816896 | tf_op jit(solution)/shard_map/reshape | solution.py:74
  8.3 10.9 %copy.113 = bf16[3,4,112,2,448]{2,3,1,0,4:T(2,128)(2,1)} copy(bf16[3,4,112,2,448]{4,3,2,1,0:T(2,128)(2,1)} %reshape.772) | data formatting | bytes 4816896 | tf_op jit(solution)/shard_map/reshape | solution.py:74
  19.3 12.0 %all-to-all-start = ((bf16[3,4,112,2,448]{2,3,1,0,4:T(2,128)(2,1)}), bf16[3,4,112,2,448]{2,3,1,0,4:T(2,128)(2,1)}, u32[]{:S(2)}, u32[]{:S(2)}) async-start(bf16[3,4,112,2,448]{2,3,1,0,4:T(2,128)(2,1)} %copy.113), calls=%async_computation | async-start | bytes 5505024 | tf_op jit(solution)/shard_map/all_to_all | solution.py:75
  31.7 23.8 %gather_fusion = f32[12544,6]{1,0:T(8,128)} fusion(f32[6,256]{0,1:T(8,128)S(1)} %copy.109, s32[13312]{0:T(1024)S(1)} %pad_clamp_fusion), kind=kCustom, calls=%fused_computation | custom fusion | bytes 652288 | tf_op jit(solution)/shard_map/jit(_take)/gather | solution.py:44
  55.5 4.8 %copy.110 = f32[7,7,256,6]{2,1,0,3:T(8,128)S(1)} copy(f32[7,7,256,6]{3,2,1,0:T(8,128)} %bitcast.112) | data formatting | bytes 602112 | tf_op jit(solution)/shard_map/jit(_take)/gather | solution.py:44
  61.5 1.0 mul.482
  63.4 1.0 mul.487
  64.5 1.1 mul.492
  65.6 1.0 mul.497
  66.7 1.0 mul.502
  67.8 1.0 mul.475
  68.8 1.2 fusion.36
  70.9 25.4 %all-to-all-done = bf16[3,4,112,2,448]{2,3,1,0,4:T(2,128)(2,1)} async-done(((bf16[3,4,112,2,448]{2,3,1,0,4:T(2,128)(2,1)}), bf16[3,4,112,2,448]{2,3,1,0,4:T(2,128)(2,1)}, u32[]{:S(2)}, u32[]{:S(2)}) %all-to-all-start) | async-done | bytes 2408480 | tf_op jit(solution)/shard_map/all_to_all | solution.py:75
  96.3 3.0 copy.115
  99.4 1.5 fusion.8
  103.2 1.1 add_convert_fusion.2
  104.3 2.8 fusion.7
  107.2 8.6 %copy.124 = bf16[3,256,112,2,7]{2,3,4,0,1:T(2,128)(2,1)} copy(bf16[3,256,112,2,7]{1,2,4,0,3:T(8,128)(2,1)} %fusion.7) | data formatting | bytes 4816896 | tf_op jit(solution)/shard_map/convert_element_type | solution.py:90
  115.8 69.9 %all_to_all.45 = bf16[3,256,112,2,7]{2,3,4,0,1:T(2,128)(2,1)S(1)} all-to-all(bf16[3,256,112,2,7]{2,3,4,0,1:T(2,128)(2,1)} %copy.124), channel_id=1, replica_groups=mesh['pb'=64,'col'=4] {'pb'}, dimensions={1} | all-to-all | bytes 4816896 | tf_op jit(solution)/shard_map/all_to_all | solution.py:91
  187.0 3.3 copy.126
  190.4 7.2 %copy.127 = f32[3,4,112,896]{3,2,1,0:T(8,128)} copy(f32[3,4,112,896]{2,1,3,0:T(4,128)} %bitcast.109) | data formatting | bytes 9633792 | tf_op jit(solution)/shard_map/convert_element_type | solution.py:93
  197.5 3.6 %fusion = bf16[3,4,112,896]{3,2,1,0:T(8,128)(2,1)S(1)} fusion(f32[3,4,112,896]{3,2,1,0:T(8,128)} %copy.127, bf16[3,4,112,896]{3,2,1,0:T(8,128)(2,1)} %param.4), kind=kLoop, calls=%fused_computation.4 | loop fusion | flops 3612672 | bytes 9633792 | tf_op jit(solution)/shard_map/convert_element_type | solution.py:93
  201.4 64.0 %all_to_all.46 = bf16[3,4,112,896]{3,2,0,1:T(8,128)(2,1)S(1)} all-to-all(bf16[3,4,112,896]{3,2,0,1:T(8,128)(2,1)S(1)} %copy.128), channel_id=1, replica_groups=mesh['pb'=64,'col'=4] {'col'}, dimensions={1} | all-to-all | bytes 4816896 | tf_op jit(solution)/shard_map/all_to_all | solution.py:96
  265.6 1.7 fusion.9
  267.2 1.6 fusion.11
  268.8 1.7 fusion.20
  270.5 1.7 fusion.18
  272.2 1.5 fusion.4
  274.6 2.1 copy.130
  276.6 78.2 %all_to_all.47 = bf16[3,1,448,896]{3,0,1,2:T(4,128)(2,1)S(1)} all-to-all(bf16[3,1,448,896]{3,0,1,2:T(4,128)(2,1)S(1)} %copy.130), channel_id=1, replica_groups=mesh['pb'=64,'col'=4] {'col'}, dimensions={2} | all-to-all | bytes 4816896 | tf_op jit(solution)/shard_map/all_to_all | solution.py:105
  355.1 1.4 copy-done.1
  356.5 2.0 fusion.1
  (67 shorter events, 8.8 us)
Async XLA Ops:
  0.0 265.6 %copy-start = (bf16[3,1,448,896]{3,2,1,0:T(8,128)(2,1)S(1)}, bf16[3,1,448,896]{3,2,1,0:T(8,128)(2,1)}, u32[]{:S(2)}) copy-start(bf16[3,1,448,896]{3,2,1,0:T(8,128)(2,1)} %param.5) | copy-start | bytes 7225348
  19.3 12.0 %copy-start.17 = (s32[7,3]{0,1:T(4,128)S(1)}, s32[7,3]{0,1:T(4,128)}, u32[]{:S(2)}) copy-start(s32[7,3]{0,1:T(4,128)} %param.7) | copy-start | bytes 256
  19.3 12.3 %copy-start.16 = (f32[6,256]{1,0:T(8,128)S(1)}, f32[6,256]{1,0:T(8,128)}, u32[]{:S(2)}) copy-start(f32[6,256]{1,0:T(8,128)} %param.6) | copy-start | bytes 18436
  19.3 77.0 %all-to-all-start = ((bf16[3,4,112,2,448]{2,3,1,0,4:T(2,128)(2,1)}), bf16[3,4,112,2,448]{2,3,1,0,4:T(2,128)(2,1)}, u32[]{:S(2)}, u32[]{:S(2)}) async-start(bf16[3,4,112,2,448]{2,3,1,0,4:T(2,128)(2,1)} %copy.113), calls=%async_computation | async-start | bytes 5505024 | tf_op jit(solution)/shard_map/all_to_all | solution.py:75
  31.3 29.1 %copy-start.14 = (s32[256]{0:T(256)}, s32[256]{0:T(256)S(1)}, u32[]{:S(2)}) copy-start(s32[256]{0:T(256)S(1)} %and_select_fusion.3) | copy-start | bytes 3076
  31.3 29.1 %copy-start.10 = (s32[256]{0:T(256)}, s32[256]{0:T(256)S(1)}, u32[]{:S(2)}) copy-start(s32[256]{0:T(256)S(1)} %get-tuple-element.29) | copy-start | bytes 3076
  31.3 29.1 %copy-start.12 = (s32[256]{0:T(256)}, s32[256]{0:T(256)S(1)}, u32[]{:S(2)}) copy-start(s32[256]{0:T(256)S(1)} %get-tuple-element.30) | copy-start | bytes 3076
  66.6 2.2 copy-start.11
  66.6 2.2 copy-start.13
  66.6 2.2 copy-start.15
  100.8 1.1 copy-start.2
  100.8 1.4 copy-start.3
  100.9 1.6 copy-start.4
  100.9 1.8 copy-start.5
  100.9 2.1 copy-start.6
  100.9 2.3 copy-start.7
  103.2 1.1 copy-start.8
  103.2 1.1 copy-start.9
  354.8 1.7 copy-start.1
where the time goes:
time: 360 us; the launch traced here: 359 us
  blocking collectives  212 us (59%)
  local copies, waits for them, and re-layouts  84.8 us (24%)
  waiting for transfers between devices  25.4 us (7%)
  other arithmetic  13 us (4%)
  starting transfers between devices  12 us (3%)
  matrix products  10.9 us (3%)
    all_to_all x1, blocking collectives, per_device(): lax.all_to_all(increment, 'col', split_axis=2, concat_axis=1, tiled=True)  78.2 us
    all_to_all x1, blocking collectives, per_device(): lax.all_to_all(projected, 'pb', split_axis=1, concat_axis=4, tiled=True)  69.9 us
    all_to_all x1, blocking collectives, per_device(): lax.all_to_all(united_rows, 'col', split_axis=1, concat_axis=2, tiled=True)  64 us
    gather x2, local copies, waits for them, and re-layouts, shifted_weights(): return jnp.take(mixing, flat_slot, axis=1)  28.6 us
    all_to_all x1, waiting for transfers between devices, per_device(): lax.all_to_all(split_cols, 'pb', split_axis=4, concat_axis=1, tiled=True)  25.4 us
    reshape x2, local copies, waits for them, and re-layouts, per_device(): split_cols = vertex.reshape(3, mesh_z, row_count, 2, full_order)  19.3 us
    all_to_all x1, starting transfers between devices, per_device(): lax.all_to_all(split_cols, 'pb', split_axis=4, concat_axis=1, tiled=True)  12 us
    convert_element_type x2, local copies, waits for them, and re-layouts, per_device(): returned_proj.astype(jnp.float32)  10.5 us
  transfers between devices with their start and end apart: 1, of which 1 were waited for; matrix products, arithmetic and copies ran while one was open for 11% of the time, Pallas kernels for 0%

commit v1 on v0

--- a/solution.py
+++ b/solution.py
@@ -93,7 +93,12 @@
     united_rows = (vertex.astype(jnp.float32) + returned_proj.astype(jnp.float32)).astype(
         jnp.bfloat16
     )
-    united = lax.all_to_all(united_rows, "col", split_axis=1, concat_axis=2, tiled=True)
+    united = jnp.concatenate(
+        lax.all_to_all(
+            jnp.stack(jnp.split(united_rows, lax.axis_size("col"), axis=1)), "col", 0, 0
+        ),
+        axis=2,
+    )
     local_q = united.shape[1]
     flat_united = united.reshape(3 * local_q, full_order, 2 * full_order)
     flat_loops = loop_blocks.reshape(3 * local_q, full_order, 2 * full_order)

time: 360 us -> 390 us (1.083)
  the two profiles are of different devices: /device:TPU:32 before, /device:TPU:38 now
where the time goes in v1:
time: 390 us; the launch traced here: 389 us
  blocking collectives  143 us (37%)
  local copies, waits for them, and re-layouts  118 us (30%)
  waiting for transfers between devices  79.7 us (20%)
  starting transfers between devices  20.1 us (5%)
  other arithmetic  16.9 us (4%)
  matrix products  10.9 us (3%)
    all_to_all x1, blocking collectives, per_device(): lax.all_to_all(increment, 'col', split_axis=2, concat_axis=1, tiled=True)  78.4 us
    all_to_all x1, blocking collectives, per_device(): lax.all_to_all(jnp.stack(jnp.split(united_rows, lax.axis_size('col'), axi...  64.2 us
    all_to_all x1, waiting for transfers between devices, per_device(): lax.all_to_all(projected, 'pb', split_axis=1, concat_axis=4, tiled=True)  56.3 us
    gather x2, local copies, waits for them, and re-layouts, shifted_weights(): return jnp.take(mixing, flat_slot, axis=1)  28.8 us
    all_to_all x1, waiting for transfers between devices, per_device(): lax.all_to_all(split_cols, 'pb', split_axis=4, concat_axis=1, tiled=True)  23.4 us
    split x5, local copies, waits for them, and re-layouts, per_device(): jnp.split(united_rows, lax.axis_size('col'), axis=1)  22.7 us
    reshape x2, local copies, waits for them, and re-layouts, per_device(): split_cols = vertex.reshape(3, mesh_z, row_count, 2, full_order)  19.3 us
    all_to_all x1, starting transfers between devices, per_device(): lax.all_to_all(split_cols, 'pb', split_axis=4, concat_axis=1, tiled=True)  12.1 us
  transfers between devices with their start and end apart: 2, of which 2 were waited for; matrix products, arithmetic and copies ran while one was open for 12% of the time, Pallas kernels for 0%

profile of v1, /device:TPU:38, one launch (start us, length us, event | category | flops | bytes accessed | tf_op | source)
XLA Modules:
  0.0 388.5 jit_solution(7275121328408365513)
XLA Ops:
  0.0 8.3 %reshape.768 = bf16[3,4,112,2,448]{4,3,2,1,0:T(2,128)(2,1)} reshape(bf16[3,4,112,896]{3,2,1,0:T(8,128)(2,1)} %param.4) | data formatting | bytes 4816896 | tf_op jit(solution)/shard_map/reshape | solution.py:74
  8.3 11.0 %copy.201 = bf16[3,4,112,2,448]{2,3,1,0,4:T(2,128)(2,1)} copy(bf16[3,4,112,2,448]{4,3,2,1,0:T(2,128)(2,1)} %reshape.768) | data formatting | bytes 4816896 | tf_op jit(solution)/shard_map/reshape | solution.py:74
  19.3 12.1 %all-to-all-start = ((bf16[3,4,112,2,448]{2,3,1,0,4:T(2,128)(2,1)}), bf16[3,4,112,2,448]{2,3,1,0,4:T(2,128)(2,1)}, u32[]{:S(2)}, u32[]{:S(2)}) async-start(bf16[3,4,112,2,448]{2,3,1,0,4:T(2,128)(2,1)} %copy.201), calls=%async_computation | async-start | bytes 5505024 | tf_op jit(solution)/shard_map/all_to_all | solution.py:75
  31.9 23.9 %gather_fusion = f32[12544,6]{1,0:T(8,128)} fusion(f32[6,256]{0,1:T(8,128)S(1)} %copy.197, s32[13312]{0:T(1024)S(1)} %pad_clamp_fusion), kind=kCustom, calls=%fused_computation | custom fusion | bytes 652288 | tf_op jit(solution)/shard_map/jit(_take)/gather | solution.py:44
  55.8 4.8 %copy.198 = f32[7,7,256,6]{2,1,0,3:T(8,128)S(1)} copy(f32[7,7,256,6]{3,2,1,0:T(8,128)} %bitcast.118) | data formatting | bytes 602112 | tf_op jit(solution)/shard_map/jit(_take)/gather | solution.py:44
  71.3 23.4 %all-to-all-done = bf16[3,4,112,2,448]{2,3,1,0,4:T(2,128)(2,1)} async-done(((bf16[3,4,112,2,448]{2,3,1,0,4:T(2,128)(2,1)}), bf16[3,4,112,2,448]{2,3,1,0,4:T(2,128)(2,1)}, u32[]{:S(2)}, u32[]{:S(2)}) %all-to-all-start) | async-done | bytes 2408480 | tf_op jit(solution)/shard_map/all_to_all | solution.py:75
  94.7 3.0 copy.203
  97.7 1.5 fusion.8
  102.7 2.8 fusion.7
  105.5 8.6 %copy.212 = bf16[3,256,112,2,7]{2,3,4,0,1:T(2,128)(2,1)} copy(bf16[3,256,112,2,7]{1,2,4,0,3:T(8,128)(2,1)} %fusion.7) | data formatting | bytes 4816896 | tf_op jit(solution)/shard_map/convert_element_type | solution.py:90
  114.1 8.0 %all-to-all-start.1 = ((bf16[3,256,112,2,7]{2,3,4,0,1:T(2,128)(2,1)}), bf16[3,256,112,2,7]{2,3,4,0,1:T(2,128)(2,1)}, u32[]{:S(2)}, u32[]{:S(2)}) async-start(bf16[3,256,112,2,7]{2,3,4,0,1:T(2,128)(2,1)} %copy.212), calls=%async_computation.1 | async-start | bytes 5505024 | tf_op jit(solution)/shard_map/all_to_all | solution.py:91
  122.1 5.7 %copy.196 = bf16[3,4,112,896]{2,1,3,0:T(4,128)(2,1)} copy(bf16[3,4,112,896]{3,2,1,0:T(8,128)(2,1)} %param.4) | data formatting | bytes 4816896 | tf_op args[0]
  127.8 56.3 %all-to-all-done.1 = bf16[3,256,112,2,7]{2,3,4,0,1:T(2,128)(2,1)} async-done(((bf16[3,256,112,2,7]{2,3,4,0,1:T(2,128)(2,1)}), bf16[3,256,112,2,7]{2,3,4,0,1:T(2,128)(2,1)}, u32[]{:S(2)}, u32[]{:S(2)}) %all-to-all-start.1) | async-done | bytes 2408480 | tf_op jit(solution)/shard_map/all_to_all | solution.py:91
  184.2 2.4 copy.213
  190.5 5.5 %fusion.57 = (bf16[3,1,112,896]{2,1,3,0:T(2,128)(2,1)}, bf16[3,1,112,896]{2,1,3,0:T(2,128)(2,1)}, bf16[3,1,112,896]{2,1,3,0:T(2,128)(2,1)}, bf16[3,1,112,896]{2,1,3,0:T(2,128)(2,1)}) fusion(bf16[3,4,112,896]{2,1,3,0:T(4,128)(2,1)S(1)} %fusion), kind=kLoop, calls=%fused_computation.133 | loop fusion | bytes 4816896 | tf_op jit(solution)/shard_map/split | solution.py:98
  195.9 3.5 copy.215
  199.4 4.6 %copy.218 = bf16[3,1,112,896]{3,2,0,1:T(8,128)(2,1)} copy(bf16[3,1,112,896]{2,1,3,0:T(2,128)(2,1)} %get-tuple-element.11) | data formatting | bytes 1204224 | tf_op jit(solution)/shard_map/split | solution.py:98
  204.0 4.6 %copy.217 = bf16[3,1,112,896]{3,2,0,1:T(8,128)(2,1)} copy(bf16[3,1,112,896]{2,1,3,0:T(2,128)(2,1)} %get-tuple-element.12) | data formatting | bytes 1204224 | tf_op jit(solution)/shard_map/split | solution.py:98
  208.6 4.6 %copy.216 = bf16[3,1,112,896]{3,2,0,1:T(8,128)(2,1)} copy(bf16[3,1,112,896]{2,1,3,0:T(2,128)(2,1)} %get-tuple-element.13) | data formatting | bytes 1204224 | tf_op jit(solution)/shard_map/split | solution.py:98
  213.1 1.8 pad_maximum_fusion.1
  214.9 64.2 %all_to_all.41 = bf16[4,3,1,112,896]{4,3,1,2,0:T(8,128)(2,1)S(1)} all-to-all(bf16[4,3,1,112,896]{4,3,1,2,0:T(8,128)(2,1)S(1)} %pad_maximum_fusion.1), channel_id=1, replica_groups=mesh['pb'=64,'col'=4] {'col'}, dimensions={0} | all-to-all | bytes 4816896 | tf_op jit(solution)/shard_map/all_to_all | solution.py:97
  279.3 1.7 fusion.9
  281.0 1.6 fusion.11
  282.6 1.7 fusion.20
  284.2 1.7 fusion.18
  285.9 1.5 fusion.4
  288.3 2.1 copy.220
  290.4 78.4 %all_to_all.42 = bf16[3,1,448,896]{3,0,1,2:T(4,128)(2,1)S(1)} all-to-all(bf16[3,1,448,896]{3,0,1,2:T(4,128)(2,1)S(1)} %copy.220), channel_id=1, replica_groups=mesh['pb'=64,'col'=4] {'col'}, dimensions={2} | all-to-all | bytes 4816896 | tf_op jit(solution)/shard_map/all_to_all | solution.py:110
  368.7 1.7 copy.221
  370.5 6.0 %copy.222 = f32[3,4,112,896]{2,1,3,0:T(4,128)} copy(bf16[3,4,112,896]{3,2,1,0:T(8,128)(2,1)} %bitcast.117) | data formatting | bytes 7225344 | tf_op jit(solution)/shard_map/convert_element_type | solution.py:111
  376.4 6.4 %fusion.1 = bf16[3,4,112,896]{2,1,3,0:T(4,128)(2,1)} fusion(f32[3,4,112,896]{2,1,3,0:T(4,128)} %copy.222, bf16[3,4,112,896]{2,1,3,0:T(4,128)(2,1)} %copy.196), kind=kLoop, calls=%fused_computation.4 | loop fusion | flops 3612672 | bytes 9633792 | tf_op jit(solution)/shard_map/convert_element_type | solution.py:111
  382.8 5.7 %copy.223 = bf16[3,4,112,896]{3,2,1,0:T(8,128)(2,1)} copy(bf16[3,4,112,896]{2,1,3,0:T(4,128)(2,1)} %fusion.1) | data formatting | bytes 4816896 | tf_op jit(solution)/shard_map/convert_element_type | solution.py:111
  (75 shorter events, 19.2 us)
Async XLA Ops:
  0.0 279.3 %copy-start = (bf16[3,1,448,896]{3,2,1,0:T(8,128)(2,1)S(1)}, bf16[3,1,448,896]{3,2,1,0:T(8,128)(2,1)}, u32[]{:S(2)}) copy-start(bf16[3,1,448,896]{3,2,1,0:T(8,128)(2,1)} %param.5) | copy-start | bytes 7225348
  19.3 12.1 %copy-start.17 = (s32[7,3]{0,1:T(4,128)S(1)}, s32[7,3]{0,1:T(4,128)}, u32[]{:S(2)}) copy-start(s32[7,3]{0,1:T(4,128)} %param.7) | copy-start | bytes 256
  19.3 12.4 %copy-start.16 = (f32[6,256]{1,0:T(8,128)S(1)}, f32[6,256]{1,0:T(8,128)}, u32[]{:S(2)}) copy-start(f32[6,256]{1,0:T(8,128)} %param.6) | copy-start | bytes 18436
  19.3 75.3 %all-to-all-start = ((bf16[3,4,112,2,448]{2,3,1,0,4:T(2,128)(2,1)}), bf16[3,4,112,2,448]{2,3,1,0,4:T(2,128)(2,1)}, u32[]{:S(2)}, u32[]{:S(2)}) async-start(bf16[3,4,112,2,448]{2,3,1,0,4:T(2,128)(2,1)} %copy.201), calls=%async_computation | async-start | bytes 5505024 | tf_op jit(solution)/shard_map/all_to_all | solution.py:75
  31.4 29.3 %copy-start.14 = (s32[256]{0:T(256)}, s32[256]{0:T(256)S(1)}, u32[]{:S(2)}) copy-start(s32[256]{0:T(256)S(1)} %and_select_fusion.3) | copy-start | bytes 3076
  31.5 29.2 %copy-start.10 = (s32[256]{0:T(256)}, s32[256]{0:T(256)S(1)}, u32[]{:S(2)}) copy-start(s32[256]{0:T(256)S(1)} %get-tuple-element.33) | copy-start | bytes 3076
  31.5 29.2 %copy-start.12 = (s32[256]{0:T(256)}, s32[256]{0:T(256)S(1)}, u32[]{:S(2)}) copy-start(s32[256]{0:T(256)S(1)} %get-tuple-element.34) | copy-start | bytes 3076
  67.0 2.1 copy-start.11
  67.0 2.1 copy-start.13
  67.0 2.1 copy-start.15
  99.2 1.1 copy-start.2
  99.2 1.4 copy-start.3
  99.2 1.6 copy-start.4
  99.2 1.8 copy-start.5
  99.2 2.1 copy-start.6
  99.2 2.3 copy-start.7
  101.5 1.1 copy-start.8
  101.5 1.1 copy-start.9
  114.1 70.0 %all-to-all-start.1 = ((bf16[3,256,112,2,7]{2,3,4,0,1:T(2,128)(2,1)}), bf16[3,256,112,2,7]{2,3,4,0,1:T(2,128)(2,1)}, u32[]{:S(2)}, u32[]{:S(2)}) async-start(bf16[3,256,112,2,7]{2,3,4,0,1:T(2,128)(2,1)} %copy.212), calls=%async_computation.1 | async-start | bytes 5505024 | tf_op jit(solution)/shard_map/all_to_all | solution.py:91
  187.3 1.8 copy-start.1
